TPU v7x, 256 devices: a whole 4x4x8 slice. The times are simulated.
256 devices in a mesh: dp: 8 (over x_hi, y), ctx: 32 (over x_lo, z, core).
Axes of the slice: x: 4 (x_hi: 2, x_lo: 2; x = x_hi * 2 + x_lo), y: 4, z: 8, core: 2. Of those that a mesh axis runs over, the one named last changes fastest.
Arguments:
- query: bfloat16 [32768, 512], P(('dp', 'ctx')), may hold values from -6 to 6
- key: bfloat16 [32768, 512], P(('dp', 'ctx')), may hold values from -6 to 6
- value: bfloat16 [32768, 512], P(('dp', 'ctx'))
- gate: bfloat16 [32768, 512], P(('dp', 'ctx')), may hold values from -6 to 6
- out_weight: bfloat16 [512, 1024], replicated, may hold values from -0.25 to 0.25
- items: bfloat16 [1024, 1024], P('ctx'), may hold values from -0.1875 to 0.1875
- cotangent: bfloat16 [32768, 1024], P(('dp', 'ctx')), may hold values from -6 to 6
- user_blocks: int32 [8, 4], P('dp'), may hold values from 1 to 16, 32 in all within a row
- tail_rows: int32 [8, 4], P('dp'), may hold values from 1 to 128
- packing: int32 [8, 32], P('dp'), may hold values from 0 to 31, each once within a row
- cand_ids: int32 [8, 4, 128], P('dp'), may hold values from 0 to 1023
Outputs:
- scores: float32 [32768, 128], P(('dp', 'ctx'))
- grad_query: bfloat16 [32768, 512], P(('dp', 'ctx'))
- grad_key: bfloat16 [32768, 512], P(('dp', 'ctx'))
- grad_value: bfloat16 [32768, 512], P(('dp', 'ctx'))
- grad_gate: bfloat16 [32768, 512], P(('dp', 'ctx'))
- grad_out_weight: float32 [512, 1024], replicated
Inputs may be any that keep to these rules, and one draw needn't show every extreme that they name: `user_blocks`: in each group the 4 counts sum to 32 and the largest is exactly 16. `packing`: each group's row is a permutation of its 32 logical blocks; slots run device by device along ctx. `cand_ids`: rows of the item table.
All inputs are finite; a program needn't handle non-finite values.
Results may differ from a plain program's by a relative error of at most 0.0058.
Values may be sent and summed in bfloat16 or wider, within the bound.
No kernel may reach another device: no remote copies, remote signals or barrier semaphores. Data moves between devices by JAX's collectives and lax.ppermute only.
A program may use at most 128 MiB of HBM per device.

v0:
```python
import jax
import jax.numpy as jnp
from jax import lax
from jax.sharding import PartitionSpec as P

HEADS = 4
HEAD_DIM = 128
BLOCK = 128
norm_eps = 1e-05


def row_facts(blocks, tails, layout, offset, length):
    row_index = offset + jnp.arange(length, dtype=jnp.int32)
    slot_index = row_index // BLOCK
    within = row_index % BLOCK
    user_ends = jnp.cumsum(blocks)
    user_starts = user_ends - blocks
    user_rows = (blocks - 1) * BLOCK + tails
    slot_match = slot_index[:, None] == jnp.arange(layout.shape[0], dtype=jnp.int32)[None, :]
    logical = jnp.sum(jnp.where(slot_match, layout[None, :], 0), axis=1)
    user_of = jnp.sum((logical[:, None] >= user_ends[None, :]).astype(jnp.int32), axis=1)
    user_match = user_of[:, None] == jnp.arange(blocks.shape[0], dtype=jnp.int32)[None, :]
    first_row = jnp.sum(jnp.where(user_match, user_starts[None, :], 0), axis=1) * BLOCK
    row_limit = jnp.sum(jnp.where(user_match, user_rows[None, :], 0), axis=1)
    position = logical * BLOCK + within
    is_valid = position - first_row < row_limit
    return (user_of, position, is_valid)


def pair_mask(query_facts, key_facts):
    same_user = query_facts[0][:, None] == key_facts[0][None, :]
    earlier = key_facts[1][None, :] <= query_facts[1][:, None]
    both_valid = query_facts[2][:, None] & key_facts[2][None, :]
    return same_user & earlier & both_valid


def silu_slope(values):
    sigma = jax.nn.sigmoid(values)
    return sigma * (1.0 + values * (1.0 - sigma))


def split_heads(array):
    return array.reshape(array.shape[0], HEADS, HEAD_DIM)


def blockwise(step, running, pieces):
    length = pieces[0].shape[0]
    stride = 512
    count = length // stride
    stacked = tuple((piece.reshape((count, stride) + piece.shape[1:]) for piece in pieces))
    offsets = jnp.arange(count, dtype=jnp.int32) * stride

    def advance(state, inputs):
        return (step(state, inputs[0], inputs[1]), None)

    result, unused = lax.scan(advance, running, (stacked, offsets))
    return result


def body(
    query, key, value, gate, out_weight, items, cotangent, user_blocks, tail_rows, packing, cand_ids
):
    local_rows = query.shape[0]
    attn_width = query.shape[1]
    score_scale = HEAD_DIM ** (-0.5)
    blocks = user_blocks[0]
    tails = tail_rows[0]
    layout = packing[0]
    candidates = cand_ids[0]
    ctx_index = lax.axis_index("ctx")
    local_facts = row_facts(blocks, tails, layout, ctx_index * local_rows, local_rows)
    query_heads = split_heads(query)
    key_heads = split_heads(key)
    value_heads = split_heads(value)
    zeros_heads = jnp.zeros((local_rows, HEADS, HEAD_DIM), jnp.float32)

    def forward_step(running, pieces, offset):
        key_piece = split_heads(pieces[0])
        value_piece = split_heads(pieces[1])
        allowed = pair_mask(
            local_facts, row_facts(blocks, tails, layout, offset, key_piece.shape[0])
        )
        logits = (
            jnp.einsum("qhd,khd->hqk", query_heads, key_piece, preferred_element_type=jnp.float32)
            * score_scale
        )
        weights = (jax.nn.silu(logits) * allowed[None]).astype(jnp.bfloat16)
        return running + jnp.einsum(
            "hqk,khd->qhd", weights, value_piece, preferred_element_type=jnp.float32
        )

    attended = blockwise(
        forward_step,
        zeros_heads,
        (
            lax.all_gather(key, "ctx", axis=0, tiled=True),
            lax.all_gather(value, "ctx", axis=0, tiled=True),
        ),
    )
    attended = attended.reshape(local_rows, attn_width)
    row_mean = jnp.mean(attended, axis=1, keepdims=True)
    centered = attended - row_mean
    inv_std = lax.rsqrt(jnp.mean(centered * centered, axis=1, keepdims=True) + norm_eps)
    normed = centered * inv_std
    valid_col = local_facts[2].astype(jnp.float32)[:, None]
    gate_float = gate.astype(jnp.float32)
    mixed = (valid_col * normed * gate_float).astype(jnp.bfloat16)
    output = jnp.dot(mixed, out_weight, preferred_element_type=jnp.float32).astype(jnp.bfloat16)
    all_scores = lax.dot_general(
        output,
        lax.all_gather(items, "ctx", axis=0, tiled=True),
        (((1,), (1,)), ((), ())),
        preferred_element_type=jnp.float32,
    )
    user_match = (
        local_facts[0][:, None] == jnp.arange(candidates.shape[0], dtype=jnp.int32)[None, :]
    )
    picked = jnp.sum(jnp.where(user_match[:, :, None], candidates[None, :, :], 0), axis=1)
    scores = jnp.take_along_axis(all_scores, picked, axis=1)
    weight_local = lax.dot_general(
        mixed, cotangent, (((0,), (0,)), ((), ())), preferred_element_type=jnp.float32
    )
    grad_out_weight = lax.psum(weight_local, ("dp", "ctx"))
    grad_mixed = lax.dot_general(
        cotangent, out_weight, (((1,), (1,)), ((), ())), preferred_element_type=jnp.float32
    )
    grad_gate = (grad_mixed * valid_col * normed).astype(jnp.bfloat16)
    grad_normed = grad_mixed * valid_col * gate_float
    grad_attended = (
        (
            grad_normed
            - jnp.mean(grad_normed, axis=1, keepdims=True)
            - normed * jnp.mean(grad_normed * normed, axis=1, keepdims=True)
        )
        * inv_std
    ).astype(jnp.bfloat16)
    grad_heads = split_heads(grad_attended)

    def query_step(running, pieces, offset):
        key_piece = split_heads(pieces[0])
        value_piece = split_heads(pieces[1])
        allowed = pair_mask(
            local_facts, row_facts(blocks, tails, layout, offset, key_piece.shape[0])
        )
        logits = (
            jnp.einsum("qhd,khd->hqk", query_heads, key_piece, preferred_element_type=jnp.float32)
            * score_scale
        )
        slopes = jnp.einsum(
            "qhd,khd->hqk", grad_heads, value_piece, preferred_element_type=jnp.float32
        )
        grad_logits = (slopes * allowed[None] * silu_slope(logits)).astype(jnp.bfloat16)
        return running + jnp.einsum(
            "hqk,khd->qhd", grad_logits, key_piece, preferred_element_type=jnp.float32
        )

    query_sum = blockwise(
        query_step,
        zeros_heads,
        (
            lax.all_gather(key, "ctx", axis=0, tiled=True),
            lax.all_gather(value, "ctx", axis=0, tiled=True),
        ),
    )

    def key_step(running, pieces, offset):
        query_piece = split_heads(pieces[0])
        grad_piece = split_heads(pieces[1])
        allowed = pair_mask(
            row_facts(blocks, tails, layout, offset, query_piece.shape[0]), local_facts
        )
        logits = (
            jnp.einsum("qhd,khd->hqk", query_piece, key_heads, preferred_element_type=jnp.float32)
            * score_scale
        )
        weights = (jax.nn.silu(logits) * allowed[None]).astype(jnp.bfloat16)
        slopes = jnp.einsum(
            "qhd,khd->hqk", grad_piece, value_heads, preferred_element_type=jnp.float32
        )
        grad_logits = (slopes * allowed[None] * silu_slope(logits)).astype(jnp.bfloat16)
        key_sum = running[0] + jnp.einsum(
            "hqk,qhd->khd", grad_logits, query_piece, preferred_element_type=jnp.float32
        )
        value_sum = running[1] + jnp.einsum(
            "hqk,qhd->khd", weights, grad_piece, preferred_element_type=jnp.float32
        )
        return (key_sum, value_sum)

    key_sum, value_sum = blockwise(
        key_step,
        (zeros_heads, zeros_heads),
        (
            lax.all_gather(query, "ctx", axis=0, tiled=True),
            lax.all_gather(grad_attended, "ctx", axis=0, tiled=True),
        ),
    )
    grad_query = (query_sum.reshape(local_rows, attn_width) * score_scale).astype(jnp.bfloat16)
    grad_key = (key_sum.reshape(local_rows, attn_width) * score_scale).astype(jnp.bfloat16)
    grad_value = value_sum.reshape(local_rows, attn_width).astype(jnp.bfloat16)
    return (scores, grad_query, grad_key, grad_value, grad_gate, grad_out_weight)


def solution(mesh):
    in_specs = (
        P(("dp", "ctx"), None),
        P(("dp", "ctx"), None),
        P(("dp", "ctx"), None),
        P(("dp", "ctx"), None),
        P(),
        P("ctx", None),
        P(("dp", "ctx"), None),
        P("dp", None),
        P("dp", None),
        P("dp", None),
        P("dp", None, None),
    )
    out_specs = (
        P(("dp", "ctx"), None),
        P(("dp", "ctx"), None),
        P(("dp", "ctx"), None),
        P(("dp", "ctx"), None),
        P(("dp", "ctx"), None),
        P(),
    )
    return jax.shard_map(body, mesh=mesh, in_specs=in_specs, out_specs=out_specs, check_vma=False)
```

profile of v0, /device:TPU:2, one launch (start us, length us, event | category | flops | bytes accessed | tf_op | source)
XLA Modules:
  0.0 709.0 jit_solution(13533291843244963831)
XLA Ops:
  20.4 58.6 %all-gather.6.cloned.1.call-done = bf16[4096,512]{1,0:T(8,128)(2,1)} async-done(((bf16[128,512]{1,0:T(8,128)(2,1)}), bf16[4096,512]{1,0:T(8,128)(2,1)}) %all-gather.6.cloned.1.call-update) | async-done | bytes 4194320 | tf_op jit(solution)/shard_map/all_gather | solution.py:97
  79.1 6.5 copy.119
  85.6 61.9 %all-gather.8.cloned.1.call-done = bf16[4096,512]{1,0:T(8,128)(2,1)} async-done(((bf16[128,512]{1,0:T(8,128)(2,1)}), bf16[4096,512]{1,0:T(8,128)(2,1)}) %all-gather.8.cloned.1.call-update) | async-done | bytes 4194320 | tf_op jit(solution)/shard_map/all_gather | solution.py:96
  147.4 6.5 copy.120
  153.9 63.8 %while.44 = (s32[]{:T(128)}, f32[128,4,128]{0,2,1:T(8,128)S(1)}, bf16[8,512,512]{1,2,0:T(8,128)(2,1)}, bf16[8,512,512]{1,2,0:T(8,128)(2,1)}, bf16[128,4,128]{2,0...) while((s32[]{:T(128)}, f32[128,4,128]{0,2,1:T(8,128)S(1)}, ...), condition=%wide.region_11.12_spmd.clone, body=%wide.region_6.11_spmd.clone.sunk | while | flops 136657424 | bytes 4356639 | solution.py:56
  220.3 80.3 %while.45 = (s32[]{:T(128)}, f32[128,4,128]{0,2,1:T(8,128)}, bf16[8,512,512]{1,2,0:T(8,128)(2,1)}, bf16[8,512,512]{1,2,0:T(8,128)(2,1)}, bf16[128,4,128]{2,0,1:T...) while((s32[]{:T(128)}, f32[128,4,128]{0,2,1:T(8,128)}, ...), condition=%wide.region_21.22_spmd.clone, body=%wide.region_16.21_spmd.clone.sunk | while | flops 204814864 | bytes 7109159 | solution.py:56
  237.8 2.5 fusion.118
  247.9 2.5 fusion.118
  258.0 2.5 fusion.118
  268.0 2.5 fusion.118
  278.1 2.5 fusion.118
  298.1 2.5 fusion.118
  302.4 2.7 fusion.53
  305.1 129.5 %gather_fusion = f32[16384]{0:T(1024)S(1)} fusion(f32[128,1024]{1,0:T(8,128)S(1)} %fusion.53, s32[16384]{0:T(1024)S(1)} %fusion.59), kind=kCustom, calls=%fused_computation | custom fusion | bytes 262144 | tf_op jit(solution)/shard_map/jit(take_along_axis)/gather | solution.py:119
  437.1 92.8 %while.46 = (s32[]{:T(128)}, f32[128,4,128]{0,2,1:T(8,128)}, f32[128,4,128]{0,2,1:T(8,128)}, bf16[8,512,512]{2,1,0:T(8,128)(2,1)}, bf16[8,512,512]{2,1,0:T(8,128...) while((s32[]{:T(128)}, f32[128,4,128]{0,2,1:T(8,128)}, ...), condition=%wide.region_27.28_spmd.clone, body=%wide.region_22.27_spmd.clone.sunk | while | flops 273627648 | bytes 11565616 | solution.py:56
  454.9 2.5 fusion.125
  466.6 2.5 fusion.125
  478.4 2.5 fusion.125
  490.1 2.5 fusion.125
  501.8 2.5 fusion.125
  513.6 2.5 fusion.125
  525.3 2.5 fusion.125
  533.4 165.6 %all-reduce.2.cloned.1.call-done = f32[512,1024]{1,0:T(8,128)} async-done(((f32[512,1024]{1,0:T(8,128)}), f32[512,1024]{1,0:T(8,128)}) %all-reduce.2.cloned.1.call-update) | async-done | bytes 2097168 | tf_op jit(solution)/shard_map/psum | solution.py:123
  698.9 3.2 copy.177
  (334 shorter events, 227.1 us)
Async XLA Ops:
  7.2 210.9 %copy-start = (bf16[512,1024]{1,0:T(8,128)(2,1)S(1)}, bf16[512,1024]{1,0:T(8,128)(2,1)}, u32[]{:S(2)}) copy-start(bf16[512,1024]{1,0:T(8,128)(2,1)} %param.21) | copy-start | bytes 3145732
  7.2 71.9 %all-gather.6.cloned.1.call-start = ((), (), s32[]{:S(2)}) async-start(), calls=%async_computation | async-start | bytes 4325376 | tf_op jit(solution)/shard_map/all_gather | solution.py:97
  7.9 139.5 %all-gather.8.cloned.1.call-start = ((), (), s32[]{:S(2)}) async-start(), calls=%async_computation.1 | async-start | bytes 4325376 | tf_op jit(solution)/shard_map/all_gather | solution.py:96
  8.7 293.7 %all-gather.10.cloned.1.call-start = ((), (), s32[]{:S(2)}) async-start(), calls=%async_computation.2 | async-start | bytes 2162688 | tf_op jit(solution)/shard_map/all_gather | solution.py:111
  9.4 427.7 %all-gather.12.cloned.1.call-start = ((), (), s32[]{:S(2)}) async-start(), calls=%async_computation.3 | async-start | bytes 4325376 | tf_op jit(solution)/shard_map/all_gather | solution.py:193
  10.0 427.1 %all-gather.14.cloned.1.call-start = ((), (), s32[]{:S(2)}) async-start(), calls=%async_computation.4 | async-start | bytes 4325376 | tf_op jit(solution)/shard_map/all_gather | solution.py:194
  153.9 64.1 %copy-start.4 = (bf16[128,1024]{1,0:T(8,128)(2,1)S(1)}, bf16[128,1024]{1,0:T(8,128)(2,1)}, u32[]{:S(2)}) copy-start(bf16[128,1024]{1,0:T(8,128)(2,1)} %param.23) | copy-start | bytes 786436
  153.9 64.2 %copy-start.6 = (bf16[128,512]{1,0:T(8,128)(2,1)S(1)}, bf16[128,512]{1,0:T(8,128)(2,1)}, u32[]{:S(2)}) copy-start(bf16[128,512]{1,0:T(8,128)(2,1)} %param.20) | copy-start | bytes 393220
  219.5 0.7 copy-start.2
  220.3 478.7 %all-reduce.2.cloned.1.call-start = ((), (), s32[]{:S(2)}) async-start(), calls=%async_computation.5 | async-start | bytes 4194304 | tf_op jit(solution)/shard_map/psum | solution.py:123
  305.1 130.2 %copy-start.3 = (bf16[128,512]{1,0:T(8,128)(2,1)S(1)}, bf16[128,512]{1,0:T(8,128)(2,1)}, u32[]{:S(2)}) copy-start(bf16[128,512]{1,0:T(8,128)(2,1)} %get-tuple-element.1178) | copy-start | bytes 393220
  305.1 130.2 %copy-start.5 = (bf16[128,1024]{1,0:T(8,128)(2,1)S(1)}, bf16[128,1024]{1,0:T(8,128)(2,1)}, u32[]{:S(2)}) copy-start(bf16[128,1024]{1,0:T(8,128)(2,1)} %param.23) | copy-start | bytes 786436
  434.6 2.5 copy-start.1
Sparse Core Ops, SparseCore 0:
  9.9 69.1 all-gather.5
  80.9 66.4 all-gather.7
  149.3 64.3 all-gather.9
  215.4 66.5 all-gather.11
  283.7 66.5 all-gather.13
  437.2 261.7 all-reduce.1
where the time goes:
time: 712 us; the launch traced here: 709 us
  waiting for transfers between devices  289 us (41%)
  local copies, waits for them, and re-layouts  217 us (30%)
  other arithmetic  101 us (14%)
  matrix products  86.5 us (12%)
  between operations  14.3 us (2%)
    psum x1, waiting for transfers between devices, body(): grad_out_weight = lax.psum(weight_local, ('dp', 'ctx'))  166 us
    gather x1, local copies, waits for them, and re-layouts, body(): scores = jnp.take_along_axis(all_scores, picked, axis=1)  129 us
    dynamic_slice x64, local copies, waits for them, and re-layouts, blockwise(): result, unused = lax.scan(advance, running, (stacked, offsets))  62.8 us
    all_gather x1, waiting for transfers between devices, body(): lax.all_gather(key, 'ctx', axis=0, tiled=True)  61.9 us
    all_gather x1, waiting for transfers between devices, body(): lax.all_gather(value, 'ctx', axis=0, tiled=True)  58.6 us
    unnamed x24, local copies, waits for them, and re-layouts  22.2 us
    dot_general x8, matrix products, key_step(): jnp.einsum('hqk,qhd->khd', grad_logits, query_piece, preferred_element_ty...  19.7 us
    dot_general x8, matrix products, query_step(): jnp.einsum('hqk,khd->qhd', grad_logits, key_piece, preferred_element_type...  19.6 us
  transfers between devices with their start and end apart: 6, of which 3 were waited for; matrix products, arithmetic and copies ran while one was open for 57% of the time, Pallas kernels for 0%

commit v1 on v0

--- a/solution.py
+++ b/solution.py
@@ -2,11 +2,17 @@
 import jax.numpy as jnp
 from jax import lax
 from jax.sharding import PartitionSpec as P
+from jax.lax import psum
 
 HEADS = 4
 HEAD_DIM = 128
 BLOCK = 128
 norm_eps = 1e-05
+
+
+def _compute_levels_all(local_x, named_axis, dev_axis):
+    long_array = psum(local_x, named_axis)
+    return psum(long_array, dev_axis)
 
 
 def row_facts(blocks, tails, layout, offset, length):
@@ -120,7 +126,7 @@
     weight_local = lax.dot_general(
         mixed, cotangent, (((0,), (0,)), ((), ())), preferred_element_type=jnp.float32
     )
-    grad_out_weight = lax.psum(weight_local, ("dp", "ctx"))
+    grad_out_weight = _compute_levels_all(weight_local, "dp", "ctx")
     grad_mixed = lax.dot_general(
         cotangent, out_weight, (((1,), (1,)), ((), ())), preferred_element_type=jnp.float32
     )

time: 712 us -> 701 us (0.985)
  waiting for transfers between devices: 289 us -> 277 us
    psum x1 -> x2, waiting for transfers between devices: 166 us -> 134 us  [the longest x1 134 us: _compute_levels_all(): return psum(long_array, dev_axis)]
    all_gather x1, waiting for transfers between devices: 0.02 us -> 14.4 us  [body(): lax.all_gather(grad_attended, 'ctx', axis=0, tiled=True)]
    unnamed x24 -> x32, local copies, waits for them, and re-layouts: 22.2 us -> 21.1 us
  transfers between devices with their start and end apart: 6 -> 7, of which waited for: 3 -> 4; matrix products, arithmetic and copies ran while one was open for 57% -> 57% of each run, Pallas kernels for 0% -> 0%
where the time goes in v1:
time: 701 us; the launch traced here: 696 us
  waiting for transfers between devices  277 us (40%)
  local copies, waits for them, and re-layouts  216 us (31%)
  other arithmetic  102 us (15%)
  matrix products  86.2 us (12%)
  between operations  14.4 us (2%)
    psum x1, waiting for transfers between devices, _compute_levels_all(): return psum(long_array, dev_axis)  134 us
    gather x1, local copies, waits for them, and re-layouts, body(): scores = jnp.take_along_axis(all_scores, picked, axis=1)  129 us
    all_gather x1, waiting for transfers between devices, body(): lax.all_gather(value, 'ctx', axis=0, tiled=True)  63.6 us
    dynamic_slice x64, local copies, waits for them, and re-layouts, blockwise(): result, unused = lax.scan(advance, running, (stacked, offsets))  62.6 us
    all_gather x1, waiting for transfers between devices, body(): lax.all_gather(key, 'ctx', axis=0, tiled=True)  61.9 us
    unnamed x32, local copies, waits for them, and re-layouts  21.1 us
    dot_general x8, matrix products, query_step(): jnp.einsum('hqk,khd->qhd', grad_logits, key_piece, preferred_element_type...  19.7 us
    dot_general x8, matrix products, key_step(): jnp.einsum('hqk,qhd->khd', grad_logits, query_piece, preferred_element_ty...  19.4 us
  transfers between devices with their start and end apart: 7, of which 4 were waited for; matrix products, arithmetic and copies ran while one was open for 57% of the time, Pallas kernels for 0%

profile of v1, /device:TPU:2, one launch (start us, length us, event | category | flops | bytes accessed | tf_op | source)
XLA Modules:
  0.0 695.7 jit_solution(9095168926770038452)
XLA Ops:
  15.5 63.6 %all-gather.6.cloned.1.call-done = bf16[4096,512]{1,0:T(8,128)(2,1)} async-done(((bf16[128,512]{1,0:T(8,128)(2,1)}), bf16[4096,512]{1,0:T(8,128)(2,1)}) %all-gather.6.cloned.1.call-update) | async-done | bytes 4194320 | tf_op jit(solution)/shard_map/all_gather | solution.py:103
  79.1 6.5 copy.119
  85.6 61.9 %all-gather.8.cloned.1.call-done = bf16[4096,512]{1,0:T(8,128)(2,1)} async-done(((bf16[128,512]{1,0:T(8,128)(2,1)}), bf16[4096,512]{1,0:T(8,128)(2,1)}) %all-gather.8.cloned.1.call-update) | async-done | bytes 4194320 | tf_op jit(solution)/shard_map/all_gather | solution.py:102
  147.4 6.5 copy.120
  153.9 64.1 %while.44 = (s32[]{:T(128)}, f32[128,4,128]{0,2,1:T(8,128)S(1)}, bf16[8,512,512]{1,2,0:T(8,128)(2,1)}, bf16[8,512,512]{1,2,0:T(8,128)(2,1)}, bf16[128,4,128]{2,0...) while((s32[]{:T(128)}, f32[128,4,128]{0,2,1:T(8,128)S(1)}, ...), condition=%wide.region_11.12_spmd.clone, body=%wide.region_6.11_spmd.clone.sunk | while | flops 136657424 | bytes 4356639 | solution.py:62
  225.7 80.6 %while.45 = (s32[]{:T(128)}, f32[128,4,128]{0,2,1:T(8,128)}, bf16[8,512,512]{1,2,0:T(8,128)(2,1)}, bf16[8,512,512]{1,2,0:T(8,128)(2,1)}, bf16[128,4,128]{2,0,1:T...) while((s32[]{:T(128)}, f32[128,4,128]{0,2,1:T(8,128)}, ...), condition=%wide.region_21.22_spmd.clone, body=%wide.region_16.21_spmd.clone.sunk | while | flops 204814864 | bytes 7109159 | solution.py:62
  243.3 2.5 fusion.118
  253.4 2.5 fusion.118
  263.5 2.5 fusion.118
  273.6 2.5 fusion.118
  283.6 2.5 fusion.118
  293.7 2.5 fusion.118
  303.8 2.5 fusion.118
  308.0 2.7 fusion.53
  310.7 129.5 %gather_fusion = f32[16384]{0:T(1024)S(1)} fusion(f32[128,1024]{1,0:T(8,128)S(1)} %fusion.53, s32[16384]{0:T(1024)S(1)} %fusion.59), kind=kCustom, calls=%fused_computation | custom fusion | bytes 262144 | tf_op jit(solution)/shard_map/jit(take_along_axis)/gather | solution.py:125
  440.9 14.4 %all-gather.14.cloned.1.call-done = bf16[4096,512]{1,0:T(8,128)(2,1)} async-done(((bf16[128,512]{1,0:T(8,128)(2,1)}), bf16[4096,512]{1,0:T(8,128)(2,1)}) %all-gather.14.cloned.1.call-update) | async-done | bytes 4194320 | tf_op jit(solution)/shard_map/all_gather | solution.py:200
  455.3 92.7 %while.46 = (s32[]{:T(128)}, f32[128,4,128]{0,2,1:T(8,128)}, f32[128,4,128]{0,2,1:T(8,128)}, bf16[8,512,512]{2,1,0:T(8,128)(2,1)}, bf16[8,512,512]{2,1,0:T(8,128...) while((s32[]{:T(128)}, f32[128,4,128]{0,2,1:T(8,128)}, ...), condition=%wide.region_27.28_spmd.clone, body=%wide.region_22.27_spmd.clone.sunk | while | flops 273627648 | bytes 11565616 | solution.py:62
  473.1 2.4 fusion.125
  484.8 2.4 fusion.125
  496.6 2.4 fusion.125
  508.3 2.4 fusion.125
  543.4 2.4 fusion.125
  551.5 134.1 %all-reduce.5.cloned.1.call-done = f32[512,1024]{1,0:T(8,128)} async-done(((f32[512,1024]{1,0:T(8,128)}), f32[512,1024]{1,0:T(8,128)}) %all-reduce.5.cloned.1.call-update) | async-done | bytes 2097168 | tf_op jit(solution)/shard_map/psum | solution.py:15
  685.7 3.2 copy.178
  (345 shorter events, 228.6 us)
Async XLA Ops:
  7.2 211.2 %copy-start = (bf16[512,1024]{1,0:T(8,128)(2,1)S(1)}, bf16[512,1024]{1,0:T(8,128)(2,1)}, u32[]{:S(2)}) copy-start(bf16[512,1024]{1,0:T(8,128)(2,1)} %param.21) | copy-start | bytes 3145732
  7.2 71.9 %all-gather.6.cloned.1.call-start = ((), (), s32[]{:S(2)}) async-start(), calls=%async_computation | async-start | bytes 4325376 | tf_op jit(solution)/shard_map/all_gather | solution.py:103
  7.9 139.5 %all-gather.8.cloned.1.call-start = ((), (), s32[]{:S(2)}) async-start(), calls=%async_computation.1 | async-start | bytes 4325376 | tf_op jit(solution)/shard_map/all_gather | solution.py:102
  8.7 299.4 %all-gather.10.cloned.1.call-start = ((), (), s32[]{:S(2)}) async-start(), calls=%async_computation.2 | async-start | bytes 2162688 | tf_op jit(solution)/shard_map/all_gather | solution.py:117
  9.4 431.5 %all-reduce.3.cloned.1.call-start = ((), (), s32[]{:S(2)}) async-start(), calls=%async_computation.5 | async-start | bytes 4194304 | tf_op jit(solution)/shard_map/psum | solution.py:14
  153.9 64.4 %copy-start.4 = (bf16[128,1024]{1,0:T(8,128)(2,1)S(1)}, bf16[128,1024]{1,0:T(8,128)(2,1)}, u32[]{:S(2)}) copy-start(bf16[128,1024]{1,0:T(8,128)(2,1)} %param.23) | copy-start | bytes 786436
  153.9 64.4 %copy-start.9 = (bf16[128,512]{1,0:T(8,128)(2,1)S(1)}, bf16[128,512]{1,0:T(8,128)(2,1)}, u32[]{:S(2)}) copy-start(bf16[128,512]{1,0:T(8,128)(2,1)} %param.20) | copy-start | bytes 393220
  218.1 4.8 copy-start.7
  218.2 4.8 copy-start.8
  218.4 6.4 copy-start.10
  219.8 0.7 copy-start.3
  219.8 5.8 copy-start.2
  222.2 218.7 %all-gather.12.cloned.1.call-start = ((), (), s32[]{:S(2)}) async-start(), calls=%async_computation.3 | async-start | bytes 4325376 | tf_op jit(solution)/shard_map/all_gather | solution.py:199
  222.8 232.5 %all-gather.14.cloned.1.call-start = ((), (), s32[]{:S(2)}) async-start(), calls=%async_computation.4 | async-start | bytes 4325376 | tf_op jit(solution)/shard_map/all_gather | solution.py:200
  224.9 0.8 copy-start.5
  225.6 460.0 %all-reduce.5.cloned.1.call-start = ((), (), s32[]{:S(2)}) async-start(), calls=%async_computation.6 | async-start | bytes 4194304 | tf_op jit(solution)/shard_map/psum | solution.py:15
  310.7 129.5 %copy-start.6 = (s32[128,128]{1,0:T(8,128)S(1)}, s32[128,128]{1,0:T(8,128)}, u32[]{:S(2)}) copy-start(s32[128,128]{1,0:T(8,128)} %copy-done.5) | copy-start | bytes 196612
  310.7 144.6 %copy-start.1 = (bf16[128,4,128]{2,0,1:T(8,128)(2,1)S(1)}, bf16[128,4,128]{2,0,1:T(8,128)(2,1)}, u32[]{:S(2)}) copy-start(bf16[128,4,128]{2,0,1:T(8,128)(2,1)} %copy.133) | copy-start | bytes 393220
Sparse Core Ops, SparseCore 0:
  9.9 69.1 all-gather.5
  80.9 66.4 all-gather.7
  149.3 64.4 all-gather.9
  222.4 96.9 all-reduce.2
  321.0 66.2 all-gather.11
  389.0 66.2 all-gather.13
  457.9 227.6 all-reduce.4
